TPU v7x, 512 devices: a whole 4x8x8 slice. The times are simulated.
512 devices in a mesh: ta: 8 (over z), af: 8 (over y_lo, x), sa: 8 (over y_hi, core).
Axes of the slice: x: 4, y: 8 (y_hi: 4, y_lo: 2; y = y_hi * 2 + y_lo), z: 8, core: 2. Of those that a mesh axis runs over, the one named last changes fastest.
Arguments:
- blocks: bfloat16 [8, 8, 8, 4, 64, 4096], P('ta', 'af', 'sa'), may hold values from -6 to 6
- coords: int32 [8, 8, 8, 4, 3], P('ta', 'af', 'sa'), may hold values from 0 to 1, as said below
- counts: int32 [8, 8, 8], P('ta', 'af', 'sa'), may hold values from 1 to 4, as said below
- time_factor: float32 [8, 128, 256], P('ta', ('af', 'sa')), may hold values from -2.4 to 2.4
- freq_factor: float32 [8, 128, 256], P('af', ('ta', 'sa')), may hold values from -2.4 to 2.4
- subj_factor: float32 [8, 128, 256], P('sa', ('ta', 'af')), may hold values from -2.4 to 2.4
- time_velocity: float32 [8, 128, 256], P('ta', ('af', 'sa')), may hold values from -1.8 to 1.8
- freq_velocity: float32 [8, 128, 256], P('af', ('ta', 'sa')), may hold values from -1.8 to 1.8
- subj_velocity: float32 [8, 128, 256], P('sa', ('ta', 'af')), may hold values from -1.8 to 1.8
Outputs:
- new_time: float32 [8, 128, 256], P('ta', ('af', 'sa'))
- new_freq: float32 [8, 128, 256], P('af', ('ta', 'sa'))
- new_subj: float32 [8, 128, 256], P('sa', ('ta', 'af'))
- new_time_velocity: float32 [8, 128, 256], P('ta', ('af', 'sa'))
- new_freq_velocity: float32 [8, 128, 256], P('af', ('ta', 'sa'))
- new_subj_velocity: float32 [8, 128, 256], P('sa', ('ta', 'af'))
Inputs may be any that keep to these rules, and one draw needn't show every extreme that they name: `coords`: entries are 0 or 1; the 4 slots of a device name distinct positions. `counts`: some device has 4 filled slots and some has 1.
All inputs are finite; a program needn't handle non-finite values.
Results may differ from a plain program's by a relative error of at most 0.005.
Values may be sent and summed in bfloat16 or wider, within the bound.
No kernel may reach another device: no remote copies, remote signals or barrier semaphores. Data moves between devices by JAX's collectives and lax.ppermute only.
A program may use at most 64 MiB of HBM per device.

v0:
```python
import jax
import jax.numpy as jnp
from jax import lax
from jax.sharding import PartitionSpec as P

BF = 64
BS = 64


def block_terms(
    block_data, time_table, freq_table, subj_table, position, valid, freq_extent, subj_extent
):
    time_extent = block_data.shape[0]
    time_block = lax.dynamic_slice_in_dim(time_table, position[0] * time_extent, time_extent, 0)
    freq_block = lax.dynamic_slice_in_dim(freq_table, position[1] * freq_extent, freq_extent, 0)
    subj_block = lax.dynamic_slice_in_dim(subj_table, position[2] * subj_extent, subj_extent, 0)
    freq_wide = freq_block.astype(jnp.float32)
    subj_wide = subj_block.astype(jnp.float32)
    khatri = (freq_wide[:, None, :] * subj_wide[None, :, :]).astype(jnp.bfloat16)
    khatri = khatri.reshape(freq_extent * subj_extent, -1)
    approx = lax.dot_general(
        time_block, khatri, (((1,), (1,)), ((), ())), preferred_element_type=jnp.float32
    )
    observed = block_data.astype(jnp.float32)
    misfit = ((approx - observed) * valid).astype(jnp.bfloat16)
    grad_time = jnp.dot(misfit, khatri, preferred_element_type=jnp.float32)
    contracted = lax.dot_general(
        misfit, time_block, (((0,), (0,)), ((), ())), preferred_element_type=jnp.float32
    )
    contracted = contracted.reshape(freq_extent, subj_extent, -1)
    grad_freq = jnp.sum(contracted * subj_wide[None, :, :], axis=1)
    grad_subj = jnp.sum(contracted * freq_wide[:, None, :], axis=0)
    return (grad_time, grad_freq, grad_subj)


def add_rows(accumulated, block_grad, offset):
    current = lax.dynamic_slice_in_dim(accumulated, offset, block_grad.shape[0], 0)
    return lax.dynamic_update_slice_in_dim(accumulated, current + block_grad, offset, 0)


def per_device(
    blocks,
    coords,
    counts,
    time_factor,
    freq_factor,
    subj_factor,
    time_velocity,
    freq_velocity,
    subj_velocity,
):
    time_table = lax.all_gather(time_factor.astype(jnp.bfloat16), ("af", "sa"), axis=1, tiled=True)[
        0
    ]
    freq_table = lax.all_gather(freq_factor.astype(jnp.bfloat16), ("ta", "sa"), axis=1, tiled=True)[
        0
    ]
    subj_table = lax.all_gather(subj_factor.astype(jnp.bfloat16), ("ta", "af"), axis=1, tiled=True)[
        0
    ]
    local_blocks = blocks[0, 0, 0]
    local_coords = coords[0, 0, 0]
    filled = counts[0, 0, 0]
    time_extent = local_blocks.shape[1]
    freq_extent = BF
    subj_extent = BS

    def visit_slot(slot_index, running, valid):
        position = local_coords[slot_index]
        grad_time, grad_freq, grad_subj = block_terms(
            local_blocks[slot_index],
            time_table,
            freq_table,
            subj_table,
            position,
            valid,
            freq_extent,
            subj_extent,
        )
        return (
            add_rows(running[0], grad_time, position[0] * time_extent),
            add_rows(running[1], grad_freq, position[1] * freq_extent),
            add_rows(running[2], grad_subj, position[2] * subj_extent),
        )

    initial = (
        jnp.zeros(time_table.shape, jnp.float32),
        jnp.zeros(freq_table.shape, jnp.float32),
        jnp.zeros(subj_table.shape, jnp.float32),
    )
    running = lax.fori_loop(
        0,
        local_blocks.shape[0],
        lambda slot_index, running: visit_slot(
            slot_index, running, (slot_index < filled).astype(jnp.float32)
        ),
        initial,
    )
    time_grad = lax.psum_scatter(running[0][None], ("af", "sa"), scatter_dimension=1, tiled=True)
    freq_grad = lax.psum_scatter(running[1][None], ("ta", "sa"), scatter_dimension=1, tiled=True)
    subj_grad = lax.psum_scatter(running[2][None], ("ta", "af"), scatter_dimension=1, tiled=True)
    new_time_velocity = 0.9 * time_velocity + time_grad / 64.0
    new_freq_velocity = 0.9 * freq_velocity + freq_grad / 64.0
    new_subj_velocity = 0.9 * subj_velocity + subj_grad / 64.0
    new_time = time_factor - 0.5 * new_time_velocity
    new_freq = freq_factor - 0.5 * new_freq_velocity
    new_subj = subj_factor - 0.5 * new_subj_velocity
    return (new_time, new_freq, new_subj, new_time_velocity, new_freq_velocity, new_subj_velocity)


def solution(mesh):
    return jax.shard_map(
        per_device,
        mesh=mesh,
        in_specs=(
            P("ta", "af", "sa", None, None, None),
            P("ta", "af", "sa", None, None),
            P("ta", "af", "sa"),
            P("ta", ("af", "sa"), None),
            P("af", ("ta", "sa"), None),
            P("sa", ("ta", "af"), None),
            P("ta", ("af", "sa"), None),
            P("af", ("ta", "sa"), None),
            P("sa", ("ta", "af"), None),
        ),
        out_specs=(
            P("ta", ("af", "sa"), None),
            P("af", ("ta", "sa"), None),
            P("sa", ("ta", "af"), None),
            P("ta", ("af", "sa"), None),
            P("af", ("ta", "sa"), None),
            P("sa", ("ta", "af"), None),
        ),
        check_vma=False,
    )
```

profile of v0, /device:TPU:2, one launch (start us, length us, event | category | flops | bytes accessed | tf_op | source)
XLA Modules:
  0.0 1572.2 jit_solution(18307715518159447462)
XLA Ops:
  7.2 0.0 all-reduce.7.cloned.1.call-start
  7.2 0.8 copy.20
  8.0 0.7 copy.41
  8.7 71.2 %all_gather.9 = bf16[1,128,256]{2,0,1:T(2,128)(2,1)S(1)} all-gather(bf16[1,2,256]{2,0,1:T(2,128)(2,1)S(1)} %copy.41), channel_id=1, replica_groups=mesh['ta'=8,'af'=8,'sa'=8] {'af','sa'}, dimensions={1}, use_global_device_ids=true | all-gather | bytes 66560 | tf_op jit(solution)/shard_map/all_gather | solution.py:52
  79.9 0.7 copy.40
  80.6 88.1 %all_gather.10 = bf16[1,128,256]{2,0,1:T(2,128)(2,1)S(1)} all-gather(bf16[1,2,256]{2,0,1:T(2,128)(2,1)S(1)} %copy.40), channel_id=1, replica_groups=mesh['ta'=8,'af'=8,'sa'=8] {'ta','sa'}, dimensions={1}, use_global_device_ids=true | all-gather | bytes 66560 | tf_op jit(solution)/shard_map/all_gather | solution.py:55
  168.7 0.7 copy.39
  169.4 155.6 %all_gather.11 = bf16[1,128,256]{2,0,1:T(2,128)(2,1)S(1)} all-gather(bf16[1,2,256]{2,0,1:T(2,128)(2,1)S(1)} %copy.39), channel_id=1, replica_groups=mesh['ta'=8,'af'=8,'sa'=8] {'ta','af'}, dimensions={1}, use_global_device_ids=true | all-gather | bytes 66560 | tf_op jit(solution)/shard_map/all_gather | solution.py:58
  325.1 30.4 %while.17 = (s32[]{:T(128)}, f32[128,256]{1,0:T(8,128)S(1)}, f32[128,256]{1,0:T(8,128)S(1)}, f32[128,256]{1,0:T(8,128)S(1)}, s32[4,3]{1,0:T(4,128)S(1)}, /*index...) while((s32[]{:T(128)}, f32[128,256]{1,0:T(8,128)S(1)}, ...), condition=%wide.region_3.0_spmd, body=%wide.region_0.0_spmd.sunk | while | flops 410042368 | bytes 17957244 | solution.py:91
  325.1 0.6 fusion.32
  327.7 0.7 multiply_convert_fusion.2
  329.1 1.8 fusion.33
  330.9 0.5 fusion.34
  331.3 0.8 multiply_reduce_fusion.4
  332.1 0.5 multiply_reduce_fusion.5
  332.7 0.6 fusion.32
  335.3 0.7 multiply_convert_fusion.2
  336.7 1.8 fusion.33
  338.5 0.5 fusion.34
  338.9 0.8 multiply_reduce_fusion.4
  339.7 0.5 multiply_reduce_fusion.5
  340.3 0.6 fusion.32
  342.9 0.7 multiply_convert_fusion.2
  344.3 1.8 fusion.33
  346.1 0.5 fusion.34
  346.5 0.8 multiply_reduce_fusion.4
  347.3 0.5 multiply_reduce_fusion.5
  347.9 0.6 fusion.32
  350.5 0.7 multiply_convert_fusion.2
  351.9 1.8 fusion.33
  353.7 0.5 fusion.34
  354.2 0.8 multiply_reduce_fusion.4
  354.9 0.5 multiply_reduce_fusion.5
  355.5 0.6 copy-done
  356.2 0.0 all-reduce.7.cloned.1.call-update
  356.2 0.0 all-reduce.9.cloned.1.call-start
  356.2 0.7 all-reduce.9.cloned.1.call-update
  356.9 0.0 all-reduce.11.cloned.1.call-start
  357.0 0.7 all-reduce.11.cloned.1.call-update
  357.7 1.3 dynamic-slice
  358.9 1.3 dynamic-slice.2
  361.5 1.3 dynamic-slice.4
  363.4 171.6 %all-reduce.7.cloned.1.call-done = f32[1,128,256]{2,1,0:T(8,128)} async-done(((f32[1,128,256]{2,1,0:T(8,128)}), f32[1,128,256]{2,1,0:T(8,128)}) %all-reduce.7.cloned.1.call-update) | async-done | bytes 131088
  535.0 1.3 multiply_subtract_fusion.2
  536.3 490.8 %all-reduce.9.cloned.1.call-done = f32[1,128,256]{2,1,0:T(8,128)} async-done(((f32[1,128,256]{2,1,0:T(8,128)}), f32[1,128,256]{2,1,0:T(8,128)}) %all-reduce.9.cloned.1.call-update) | async-done | bytes 131088
  1027.1 1.3 multiply_subtract_fusion.1
  1028.4 535.9 %all-reduce.11.cloned.1.call-done = f32[1,128,256]{2,1,0:T(8,128)} async-done(((f32[1,128,256]{2,1,0:T(8,128)}), f32[1,128,256]{2,1,0:T(8,128)}) %all-reduce.11.cloned.1.call-update) | async-done | bytes 131088
  1564.4 1.3 multiply_subtract_fusion
  (39 shorter events, 0.3 us)
Async XLA Ops:
  7.2 527.8 %all-reduce.7.cloned.1.call-start = ((), (), s32[]{:S(2)}) async-start(), calls=%async_computation | async-start | bytes 262144
  325.0 210.0 %copy-start.3 = (f32[1,2,256]{2,1,0:T(2,128)S(1)}, f32[1,2,256]{2,1,0:T(2,128)}, u32[]{:S(2)}) copy-start(f32[1,2,256]{2,1,0:T(2,128)} %param.14) | copy-start | bytes 6148
  325.0 210.0 %copy-start.6 = (f32[1,2,256]{2,1,0:T(2,128)S(1)}, f32[1,2,256]{2,1,0:T(2,128)}, u32[]{:S(2)}) copy-start(f32[1,2,256]{2,1,0:T(2,128)} %param.17) | copy-start | bytes 6148
  325.0 702.1 %copy-start.4 = (f32[1,2,256]{2,1,0:T(2,128)S(1)}, f32[1,2,256]{2,1,0:T(2,128)}, u32[]{:S(2)}) copy-start(f32[1,2,256]{2,1,0:T(2,128)} %param.15) | copy-start | bytes 6148
  325.0 702.1 %copy-start.7 = (f32[1,2,256]{2,1,0:T(2,128)S(1)}, f32[1,2,256]{2,1,0:T(2,128)}, u32[]{:S(2)}) copy-start(f32[1,2,256]{2,1,0:T(2,128)} %param.18) | copy-start | bytes 6148
  325.1 1239.3 %copy-start.5 = (f32[1,2,256]{2,1,0:T(2,128)S(1)}, f32[1,2,256]{2,1,0:T(2,128)}, u32[]{:S(2)}) copy-start(f32[1,2,256]{2,1,0:T(2,128)} %param.16) | copy-start | bytes 6148
  325.1 1239.3 %copy-start.8 = (f32[1,2,256]{2,1,0:T(2,128)S(1)}, f32[1,2,256]{2,1,0:T(2,128)}, u32[]{:S(2)}) copy-start(f32[1,2,256]{2,1,0:T(2,128)} %param.19) | copy-start | bytes 6148
  355.5 0.6 copy-start
  355.5 0.7 copy-start.1
  355.5 1.5 copy-start.2
  356.2 671.0 %all-reduce.9.cloned.1.call-start = ((), (), s32[]{:S(2)}) async-start(), calls=%async_computation.1 | async-start | bytes 262144
  356.9 1207.4 %all-reduce.11.cloned.1.call-start = ((), (), s32[]{:S(2)}) async-start(), calls=%async_computation.2 | async-start | bytes 262144
Sparse Core Ops, SparseCore 0:
  356.3 178.6 all-reduce.6
  537.9 489.1 all-reduce.8
  1030.3 534.0 all-reduce.10
where the time goes:
time: 1570 us
  waiting for transfers between devices  1200 us (76%)
  blocking collectives  315 us (20%)
  between operations  15.8 us (1%)
    unnamed x6, waiting for transfers between devices  1200 us
    all_gather x1, blocking collectives, per_device(): lax.all_gather(subj_factor.astype(jnp.bfloat16), ('ta', 'af'), axis=1, ti...  156 us
    all_gather x1, blocking collectives, per_device(): lax.all_gather(freq_factor.astype(jnp.bfloat16), ('ta', 'sa'), axis=1, ti...  88.1 us
    all_gather x1, blocking collectives, per_device(): lax.all_gather(time_factor.astype(jnp.bfloat16), ('af', 'sa'), axis=1, ti...  71.2 us
  transfers between devices with their start and end apart: 3, of which 3 were waited for; matrix products, arithmetic and copies ran while one was open for 0% of the time, Pallas kernels for 0%

commit v1 on v0

--- a/solution.py
+++ b/solution.py
@@ -52,9 +52,15 @@
     time_table = lax.all_gather(time_factor.astype(jnp.bfloat16), ("af", "sa"), axis=1, tiled=True)[
         0
     ]
-    freq_table = lax.all_gather(freq_factor.astype(jnp.bfloat16), ("ta", "sa"), axis=1, tiled=True)[
-        0
-    ]
+
+    def see_the_slots(panel):
+        current_value = jax.lax.axis_size(("ta", "sa"))
+        h_now = jnp.stack(current_value * [panel])
+        opened = jax.lax.all_to_all(h_now, ("ta", "sa"), 0, 0)
+        main = jnp.concatenate(opened, axis=1)
+        return main
+
+    freq_table = see_the_slots(freq_factor.astype(jnp.bfloat16))[0]
     subj_table = lax.all_gather(subj_factor.astype(jnp.bfloat16), ("ta", "af"), axis=1, tiled=True)[
         0
     ]

time: 1570 us -> 1510 us (0.962)
  blocking collectives: 315 us -> 236 us
  starting transfers between devices: 0.12 us -> 16.7 us
    all_gather x1 -> x0, blocking collectives: 88.1 us -> none  [per_device(): lax.all_gather(freq_factor.astype(jnp.bfloat16), ('ta', 'sa'), axis=1, ti...]
    all_to_all x0 -> x1, starting transfers between devices: none -> 16.6 us  [see_the_slots(): opened = jax.lax.all_to_all(h_now, ('ta', 'sa'), 0, 0)]
  transfers between devices with their start and end apart: 3 -> 4, of which waited for: 3 -> 3; matrix products, arithmetic and copies ran while one was open for 0% -> 1% of each run, Pallas kernels for 0% -> 0%
where the time goes in v1:
time: 1510 us
  waiting for transfers between devices  1200 us (79%)
  blocking collectives  236 us (16%)
  starting transfers between devices  16.7 us (1%)
  between operations  15.9 us (1%)
    unnamed x6, waiting for transfers between devices  1200 us
    all_gather x1, blocking collectives, per_device(): lax.all_gather(subj_factor.astype(jnp.bfloat16), ('ta', 'af'), axis=1, ti...  165 us
    all_gather x1, blocking collectives, per_device(): lax.all_gather(time_factor.astype(jnp.bfloat16), ('af', 'sa'), axis=1, ti...  70.7 us
  transfers between devices with their start and end apart: 4, of which 3 were waited for; matrix products, arithmetic and copies ran while one was open for 1% of the time, Pallas kernels for 0%

profile of v1, /device:TPU:2, one launch (start us, length us, event | category | flops | bytes accessed | tf_op | source)
XLA Modules:
  0.0 1507.4 jit_solution(16958666439071936763)
XLA Ops:
  7.2 0.7 convert_bitcast_fusion
  7.9 0.7 stack.2
  8.5 16.6 %all-to-all-start = ((bf16[64,1,2,256]{3,2,1,0:T(2,128)(2,1)}), bf16[64,1,2,256]{3,2,1,0:T(2,128)(2,1)S(1)}, u32[]{:S(2)}, u32[]{:S(2)}) async-start(bf16[64,1,2,256]{3,2,1,0:T(2,128)(2,1)} %stack.2), calls=%async_computation | async-start | bytes 131072 | tf_op jit(solution)/shard_map/all_to_all | solution.py:59
  25.1 0.0 all-reduce.7.cloned.1.call-start
  25.2 0.8 copy.19
  25.9 0.7 copy.35
  26.6 70.7 %all_gather.6 = bf16[1,128,256]{2,0,1:T(2,128)(2,1)S(1)} all-gather(bf16[1,2,256]{2,0,1:T(2,128)(2,1)S(1)} %copy.35), channel_id=1, replica_groups=mesh['ta'=8,'af'=8,'sa'=8] {'af','sa'}, dimensions={1}, use_global_device_ids=true | all-gather | bytes 66560 | tf_op jit(solution)/shard_map/all_gather | solution.py:52
  97.3 0.7 copy.34
  98.0 165.3 %all_gather.7 = bf16[1,128,256]{2,0,1:T(2,128)(2,1)S(1)} all-gather(bf16[1,2,256]{2,0,1:T(2,128)(2,1)S(1)} %copy.34), channel_id=1, replica_groups=mesh['ta'=8,'af'=8,'sa'=8] {'ta','af'}, dimensions={1}, use_global_device_ids=true | all-gather | bytes 66560 | tf_op jit(solution)/shard_map/all_gather | solution.py:64
  263.5 30.9 %while.17 = (s32[]{:T(128)}, f32[128,256]{1,0:T(8,128)S(1)}, f32[128,256]{1,0:T(8,128)S(1)}, f32[128,256]{1,0:T(8,128)S(1)}, s32[4,3]{1,0:T(4,128)S(1)}, /*index...) while((s32[]{:T(128)}, f32[128,256]{1,0:T(8,128)S(1)}, ...), condition=%wide.region_3.0_spmd, body=%wide.region_0.0_spmd.sunk | while | flops 410042368 | bytes 17957244 | solution.py:97
  263.5 0.6 fusion.32
  266.1 0.7 multiply_convert_fusion.2
  267.4 1.8 fusion.33
  269.2 0.5 fusion.34
  269.7 0.8 multiply_reduce_fusion.4
  270.5 0.7 multiply_reduce_fusion.5
  271.2 0.6 fusion.32
  273.8 0.7 multiply_convert_fusion.2
  275.2 1.8 fusion.33
  277.0 0.5 fusion.34
  277.4 0.8 multiply_reduce_fusion.4
  278.2 0.7 multiply_reduce_fusion.5
  278.9 0.6 fusion.32
  281.5 0.7 multiply_convert_fusion.2
  282.9 1.8 fusion.33
  284.7 0.5 fusion.34
  285.2 0.8 multiply_reduce_fusion.4
  285.9 0.7 multiply_reduce_fusion.5
  286.7 0.6 fusion.32
  289.3 0.7 multiply_convert_fusion.2
  290.6 1.8 fusion.33
  292.4 0.5 fusion.34
  292.9 0.8 multiply_reduce_fusion.4
  293.6 0.7 multiply_reduce_fusion.5
  294.4 0.6 copy-done
  295.0 0.0 all-reduce.9.cloned.1.call-start
  295.1 0.7 all-reduce.9.cloned.1.call-update
  295.8 0.0 all-reduce.11.cloned.1.call-start
  295.8 1.3 dynamic-slice
  297.1 1.3 dynamic-slice.2
  299.7 1.3 dynamic-slice.4
  301.6 0.0 all-reduce.11.cloned.1.call-update
  301.6 168.6 %all-reduce.7.cloned.1.call-done = f32[1,128,256]{2,1,0:T(8,128)} async-done(((f32[1,128,256]{2,1,0:T(8,128)}), f32[1,128,256]{2,1,0:T(8,128)}) %all-reduce.7.cloned.1.call-update) | async-done | bytes 131088
  470.2 1.3 multiply_subtract_fusion.2
  471.5 490.8 %all-reduce.9.cloned.1.call-done = f32[1,128,256]{2,1,0:T(8,128)} async-done(((f32[1,128,256]{2,1,0:T(8,128)}), f32[1,128,256]{2,1,0:T(8,128)}) %all-reduce.9.cloned.1.call-update) | async-done | bytes 131088
  962.4 1.3 multiply_subtract_fusion.1
  963.6 535.9 %all-reduce.11.cloned.1.call-done = f32[1,128,256]{2,1,0:T(8,128)} async-done(((f32[1,128,256]{2,1,0:T(8,128)}), f32[1,128,256]{2,1,0:T(8,128)}) %all-reduce.11.cloned.1.call-update) | async-done | bytes 131088
  1499.6 1.3 multiply_subtract_fusion
  (41 shorter events, 0.4 us)
Async XLA Ops:
  8.5 254.8 %all-to-all-start = ((bf16[64,1,2,256]{3,2,1,0:T(2,128)(2,1)}), bf16[64,1,2,256]{3,2,1,0:T(2,128)(2,1)S(1)}, u32[]{:S(2)}, u32[]{:S(2)}) async-start(bf16[64,1,2,256]{3,2,1,0:T(2,128)(2,1)} %stack.2), calls=%async_computation | async-start | bytes 131072 | tf_op jit(solution)/shard_map/all_to_all | solution.py:59
  25.1 445.1 %all-reduce.7.cloned.1.call-start = ((), (), s32[]{:S(2)}) async-start(), calls=%async_computation.1 | async-start | bytes 262144
  263.4 206.8 %copy-start.3 = (f32[1,2,256]{2,1,0:T(2,128)S(1)}, f32[1,2,256]{2,1,0:T(2,128)}, u32[]{:S(2)}) copy-start(f32[1,2,256]{2,1,0:T(2,128)} %param.14) | copy-start | bytes 6148
  263.4 206.8 %copy-start.6 = (f32[1,2,256]{2,1,0:T(2,128)S(1)}, f32[1,2,256]{2,1,0:T(2,128)}, u32[]{:S(2)}) copy-start(f32[1,2,256]{2,1,0:T(2,128)} %param.17) | copy-start | bytes 6148
  263.4 698.9 %copy-start.4 = (f32[1,2,256]{2,1,0:T(2,128)S(1)}, f32[1,2,256]{2,1,0:T(2,128)}, u32[]{:S(2)}) copy-start(f32[1,2,256]{2,1,0:T(2,128)} %param.15) | copy-start | bytes 6148
  263.4 698.9 %copy-start.7 = (f32[1,2,256]{2,1,0:T(2,128)S(1)}, f32[1,2,256]{2,1,0:T(2,128)}, u32[]{:S(2)}) copy-start(f32[1,2,256]{2,1,0:T(2,128)} %param.18) | copy-start | bytes 6148
  263.4 1236.1 %copy-start.5 = (f32[1,2,256]{2,1,0:T(2,128)S(1)}, f32[1,2,256]{2,1,0:T(2,128)}, u32[]{:S(2)}) copy-start(f32[1,2,256]{2,1,0:T(2,128)} %param.16) | copy-start | bytes 6148
  263.5 1236.1 %copy-start.8 = (f32[1,2,256]{2,1,0:T(2,128)S(1)}, f32[1,2,256]{2,1,0:T(2,128)}, u32[]{:S(2)}) copy-start(f32[1,2,256]{2,1,0:T(2,128)} %param.19) | copy-start | bytes 6148
  294.4 0.6 copy-start
  294.4 0.7 copy-start.1
  294.4 7.2 copy-start.2
  295.0 667.3 %all-reduce.9.cloned.1.call-start = ((), (), s32[]{:S(2)}) async-start(), calls=%async_computation.2 | async-start | bytes 262144
  295.8 1203.8 %all-reduce.11.cloned.1.call-start = ((), (), s32[]{:S(2)}) async-start(), calls=%async_computation.3 | async-start | bytes 262144
Sparse Core Ops, SparseCore 0:
  295.2 175.0 all-reduce.6
  473.1 489.1 all-reduce.8
  965.5 534.0 all-reduce.10
